TPU v7x, 32 devices: a whole 2x2x4 slice. The times are simulated.
32 devices in a mesh: rows: 8 (over z, x), tm: 4 (over y, core).
Axes of the slice: x: 2, y: 2, z: 4, core: 2. Of those that a mesh axis runs over, the one named last changes fastest.
Arguments:
- snapshots: bfloat16 [262144, 512], P('rows', 'tm'), may hold values from -6 to 6
- modes: bfloat16 [262144, 256], P('rows'), may hold values from -0.01171875 to 0.01171875
- eig_vectors: float32 [3, 256], replicated, may hold values from -0.375 to 0.375
- eig_values: float32 [3], replicated, may hold values from -1 to 1
Outputs:
- operator: float32 [256, 256], replicated
- eig_residual: float32 [3, 256], replicated
- residual_norm: float32 [3], replicated
All inputs are finite; a program needn't handle non-finite values.
Results may differ from a plain program's by a relative error of at most 0.0003.
Values may be sent and summed in bfloat16 or wider, within the bound.
A program may use at most 128 MiB of HBM per device.

v0:
```python
import jax
import jax.numpy as jnp
from jax import lax
from jax.sharding import PartitionSpec as P


def pair_terms(coords, after, keep):
    lead = coords * keep
    trail = jnp.concatenate([coords[:, 1:], after], axis=1)
    cross_part = jnp.dot(
        trail, lead.T, precision=lax.Precision.HIGHEST, preferred_element_type=jnp.float32
    )
    gram_part = jnp.dot(
        lead, lead.T, precision=lax.Precision.HIGHEST, preferred_element_type=jnp.float32
    )
    return (cross_part, gram_part)


def body(snapshots, modes, eig_vectors, eig_values):
    block_cols = snapshots.shape[1]
    width = modes.shape[1]
    time_count = lax.axis_size("tm")
    total_cols = block_cols * time_count
    partial_value = jnp.einsum("mr,mt->rt", modes, snapshots, preferred_element_type=jnp.float32)
    coords = lax.psum(partial_value, "rows")
    series = lax.all_gather(coords, "tm", axis=1, tiled=True)
    every = lax.broadcasted_iota(jnp.int32, (1, total_cols), 1)
    whole_keep = (every < total_cols - 1).astype(jnp.float32)
    zero_col = jnp.zeros((width, 1), jnp.float32)
    cross, gram = pair_terms(series, zero_col, whole_keep)
    scale = jnp.float32(total_cols - 1)
    cross = cross / scale
    gram = gram / scale + jnp.eye(width, dtype=jnp.float32)
    factor = jnp.linalg.cholesky(gram)
    operator = jax.scipy.linalg.cho_solve((factor, True), cross.T).T
    eig_residual = (
        jnp.dot(
            eig_vectors,
            operator.T,
            precision=lax.Precision.HIGHEST,
            preferred_element_type=jnp.float32,
        )
        - eig_values[:, None] * eig_vectors
    )
    residual_norm = jnp.sqrt(jnp.sum(eig_residual * eig_residual, axis=1) + 1e-06)
    return (operator, eig_residual, residual_norm)


def solution(mesh):
    return jax.shard_map(
        body,
        mesh=mesh,
        in_specs=(P("rows", "tm"), P("rows", None), P(), P()),
        out_specs=(P(), P(), P()),
        check_vma=False,
    )
```

profile of v0, /device:TPU:0, one launch (start us, length us, event | category | flops | bytes accessed | tf_op | source)
XLA Modules:
  0.0 174.0 jit_solution(5392952128399339872)
XLA Ops:
  7.2 0.0 copy-start
  7.2 0.0 copy-start.1
  7.2 0.0 all-reduce.4.cloned.1.call-start
  7.2 13.4 %fusion.23 = f32[256,128]{1,0:T(8,128)} fusion(bf16[32768,256]{1,0:T(8,128)(2,1)} %param.5, bf16[32768,128]{1,0:T(8,128)(2,1)} %param.4), kind=kOutput, calls=%fused_computation.53 | convolution fusion | flops 2147483648 | bytes 25296896 | tf_op jit(solution)/shard_map/mr,mt->rt/dot_general | solution.py:24
  20.6 0.0 all-reduce.4.cloned.1.call-update
  20.7 73.3 %all-reduce.4.cloned.1.call-done = f32[256,128]{1,0:T(8,128)} async-done(((f32[256,128]{1,0:T(8,128)}), f32[256,128]{1,0:T(8,128)}) %all-reduce.4.cloned.1.call-update) | async-done | bytes 131088 | tf_op jit(solution)/shard_map/psum | solution.py:25
  94.0 7.5 %all_gather.3 = f32[256,512]{1,0:T(8,128)S(1)} all-gather(f32[256,128]{1,0:T(8,128)} %all-reduce.4.cloned.1.call-done), channel_id=1, replica_groups=mesh['rows'=8,'tm'=4] {'tm'}, dimensions={1}, use_global_device_ids=true | all-gather | bytes 655360 | tf_op jit(solution)/shard_map/all_gather | solution.py:26
  101.5 0.2 slice.77
  101.7 0.6 convert_add_fusion
  102.4 0.6 convolution_multiply_fusion
  103.0 0.1 copy.8
  103.2 11.7 %cholesky.50 = f32[128,128]{1,0:T(8,128)S(1)} custom-call(f32[128,128]{1,0:T(8,128)S(1)} %cholesky.118), custom_call_target="Cholesky" | custom-call | tf_op jit(solution)/shard_map/jit(cholesky)/cholesky | solution.py:34
  115.0 9.8 %custom-call.18 = f32[1,128,128]{1,2,0:T(8,128)S(1)} custom-call(f32[1,128,128]{2,1,0:T(8,128)S(1)} %get-tuple-element.27), custom_call_target="InvertDiagBlocksLowerTriangular" | custom-call | tf_op jit(solution)/shard_map/jit(cholesky)/cholesky | solution.py:34
  124.8 0.2 constant_dynamic-update-slice_fusion.1
  125.0 0.3 convolution_subtract_fusion.2
  125.3 11.7 %cholesky.105 = f32[128,128]{1,0:T(8,128)S(1)} custom-call(f32[128,128]{1,0:T(8,128)S(1)} %convolution_subtract_fusion.2), custom_call_target="Cholesky" | custom-call | tf_op jit(solution)/shard_map/jit(cholesky)/cholesky | solution.py:34
  137.0 0.6 compare_reduce_fusion
  139.0 0.1 triangular_solve.72
  139.1 4.2 %while.1 = (s32[]{:T(128)}, f32[256,256]{1,0:T(8,128)S(1)}, s32[2,2]{1,0:T(2,128)S(1)}, f32[2,128,128]{2,1,0:T(8,128)S(1)}, s32[]{:T(128)}) while((s32[]{:T(128)}, f32[256,256]{1,0:T(8,128)S(1)}, s32[2,2]{1,0:T(2,128)S(1)}, f32[2,128,128]{2,1,0:T(8,128)S(1)}, s32[]{:T(128)}) %tuple.30), condition=%wide.while_cond, body=%wide.while_body.sunk | while | flops 2 | bytes 131189 | solution.py:35
  139.3 0.6 fusion.35
  139.9 1.4 bitcast_dynamic-update-slice_fusion.2
  141.3 0.6 fusion.35
  141.9 1.4 bitcast_dynamic-update-slice_fusion.2
  143.3 19.7 %custom-call.19 = f32[2,128,128]{1,2,0:T(8,128)S(1)} custom-call(f32[2,128,128]{2,1,0:T(8,128)S(1)} %get-tuple-element.10), custom_call_target="InvertDiagBlocksLowerTriangular" | custom-call | tf_op jit(solution)/shard_map/jit(_cho_solve)/triangular_solve | solution.py:35
  162.9 0.3 fusion.9
  163.3 0.4 convolution_subtract_fusion.1
  163.7 0.3 fusion.16
  164.0 0.3 fusion.15
  164.2 0.3 convolution_subtract_fusion
  164.6 0.3 fusion.14
  164.9 0.8 copy.10
  165.7 0.0 copy-done
  165.7 0.0 copy-done.1
  165.7 1.0 multiply_reduce_fusion
  166.7 0.5 add_sqrt_fusion
  (12 shorter events, 0.2 us)
Async XLA Ops:
  7.2 158.5 %copy-start = (f32[3,256]{1,0:T(4,128)S(1)}, f32[3,256]{1,0:T(4,128)}, u32[]{:S(2)}) copy-start(f32[3,256]{1,0:T(4,128)} %param.6) | copy-start | bytes 9220
  7.2 158.5 %copy-start.1 = (f32[3]{0:T(128)S(1)}, f32[3]{0:T(128)}, u32[]{:S(2)}) copy-start(f32[3]{0:T(128)} %param.7) | copy-start | bytes 40
  7.2 86.8 %all-reduce.4.cloned.1.call-start = ((), (), s32[]{:S(2)}) async-start(), calls=%async_computation | async-start | bytes 262144 | tf_op jit(solution)/shard_map/psum | solution.py:25
Sparse Core Ops, SparseCore 0:
  20.8 73.1 all-reduce.3
where the time goes:
time: 174 us
  waiting for transfers between devices  73.3 us (42%)
  other arithmetic  54.2 us (31%)
  matrix products  17.9 us (10%)
  between operations  15.5 us (9%)
  blocking collectives  7.53 us (4%)
  local copies, waits for them, and re-layouts  5.22 us (3%)
    psum x1, waiting for transfers between devices, body(): coords = lax.psum(partial_value, 'rows')  73.3 us
    another operation x6, other arithmetic, body(): factor = jnp.linalg.cholesky(gram)  33.9 us
    another operation x3, other arithmetic, body(): operator = jax.scipy.linalg.cho_solve((factor, True), cross.T).T  19.7 us
    dot_general x1, matrix products, body(): jnp.einsum('mr,mt->rt', modes, snapshots, preferred_element_type=jnp.floa...  13.4 us
    all_gather x1, blocking collectives, body(): series = lax.all_gather(coords, 'tm', axis=1, tiled=True)  7.53 us
    another operation x6, local copies, waits for them, and re-layouts  3.95 us
  transfers between devices with their start and end apart: 1, of which 1 were waited for; matrix products, arithmetic and copies ran while one was open for 0% of the time, Pallas kernels for 0%

commit v1 on v0

--- a/solution.py
+++ b/solution.py
@@ -22,7 +22,7 @@
     time_count = lax.axis_size("tm")
     total_cols = block_cols * time_count
     partial_value = jnp.einsum("mr,mt->rt", modes, snapshots, preferred_element_type=jnp.float32)
-    coords = lax.psum(partial_value, "rows")
+    coords = jnp.sum(lax.all_gather(partial_value, "rows"), axis=0)
     series = lax.all_gather(coords, "tm", axis=1, tiled=True)
     every = lax.broadcasted_iota(jnp.int32, (1, total_cols), 1)
     whole_keep = (every < total_cols - 1).astype(jnp.float32)

time: 174 us -> 145 us (0.83)
  waiting for transfers between devices: 73.3 us -> 43.1 us
    psum x1 -> x0, waiting for transfers between devices: 73.3 us -> none  [body(): coords = lax.psum(partial_value, 'rows')]
    all_gather x0 -> x1, waiting for transfers between devices: none -> 43.1 us  [body(): coords = jnp.sum(lax.all_gather(partial_value, 'rows'), axis=0)]
where the time goes in v1:
time: 145 us
  other arithmetic  55.5 us (38%)
  waiting for transfers between devices  43.1 us (30%)
  matrix products  17.9 us (12%)
  between operations  15.5 us (11%)
  blocking collectives  7.34 us (5%)
  local copies, waits for them, and re-layouts  5.22 us (4%)
    all_gather x1, waiting for transfers between devices, body(): coords = jnp.sum(lax.all_gather(partial_value, 'rows'), axis=0)  43.1 us
    another operation x6, other arithmetic, body(): factor = jnp.linalg.cholesky(gram)  33.9 us
    another operation x3, other arithmetic, body(): operator = jax.scipy.linalg.cho_solve((factor, True), cross.T).T  19.7 us
    dot_general x1, matrix products, body(): jnp.einsum('mr,mt->rt', modes, snapshots, preferred_element_type=jnp.floa...  13.4 us
    all_gather x1, blocking collectives, body(): series = lax.all_gather(coords, 'tm', axis=1, tiled=True)  7.34 us
    another operation x6, local copies, waits for them, and re-layouts  3.95 us
  transfers between devices with their start and end apart: 1, of which 1 were waited for; matrix products, arithmetic and copies ran while one was open for 0% of the time, Pallas kernels for 0%

profile of v1, /device:TPU:0, one launch (start us, length us, event | category | flops | bytes accessed | tf_op | source)
XLA Modules:
  0.0 144.9 jit_solution(623486617830757040)
XLA Ops:
  7.2 0.0 copy-start
  7.2 0.0 copy-start.1
  7.2 0.0 all-gather.3.cloned.1.call-start
  7.2 13.4 %fusion.23 = f32[256,128]{1,0:T(8,128)} fusion(bf16[32768,256]{1,0:T(8,128)(2,1)} %param.5, bf16[32768,128]{1,0:T(8,128)(2,1)} %param.4), kind=kOutput, calls=%fused_computation.53 | convolution fusion | flops 2147483648 | bytes 25296896 | tf_op jit(solution)/shard_map/mr,mt->rt/dot_general | solution.py:24
  20.6 0.0 all-gather.3.cloned.1.call-update
  20.7 43.1 %all-gather.3.cloned.1.call-done = f32[2048,128]{1,0:T(8,128)} async-done(((f32[256,128]{1,0:T(8,128)}), f32[2048,128]{1,0:T(8,128)}) %all-gather.3.cloned.1.call-update) | async-done | bytes 1048592 | tf_op jit(solution)/shard_map/all_gather | solution.py:25
  63.8 1.3 reduce_sum.18
  65.1 7.3 %all_gather.11 = f32[256,512]{1,0:T(8,128)S(1)} all-gather(f32[256,128]{1,0:T(8,128)S(1)} %reduce_sum.18), channel_id=1, replica_groups=mesh['rows'=8,'tm'=4] {'tm'}, dimensions={1}, use_global_device_ids=true | all-gather | bytes 655360 | tf_op jit(solution)/shard_map/all_gather | solution.py:26
  72.4 0.2 slice.77
  72.6 0.6 convert_add_fusion
  73.3 0.1 copy.8
  73.5 11.7 %cholesky.50 = f32[128,128]{1,0:T(8,128)S(1)} custom-call(f32[128,128]{1,0:T(8,128)S(1)} %cholesky.118), custom_call_target="Cholesky" | custom-call | tf_op jit(solution)/shard_map/jit(cholesky)/cholesky | solution.py:34
  85.2 0.6 convolution_multiply_fusion
  85.9 9.8 %custom-call.18 = f32[1,128,128]{1,2,0:T(8,128)S(1)} custom-call(f32[1,128,128]{2,1,0:T(8,128)S(1)} %get-tuple-element.27), custom_call_target="InvertDiagBlocksLowerTriangular" | custom-call | tf_op jit(solution)/shard_map/jit(cholesky)/cholesky | solution.py:34
  95.7 0.2 constant_dynamic-update-slice_fusion.1
  95.9 0.3 convolution_subtract_fusion.2
  96.2 11.7 %cholesky.105 = f32[128,128]{1,0:T(8,128)S(1)} custom-call(f32[128,128]{1,0:T(8,128)S(1)} %convolution_subtract_fusion.2), custom_call_target="Cholesky" | custom-call | tf_op jit(solution)/shard_map/jit(cholesky)/cholesky | solution.py:34
  107.9 0.6 compare_reduce_fusion
  109.9 0.1 triangular_solve.72
  110.0 4.2 %while.1 = (s32[]{:T(128)}, f32[256,256]{1,0:T(8,128)S(1)}, s32[2,2]{1,0:T(2,128)S(1)}, f32[2,128,128]{2,1,0:T(8,128)S(1)}, s32[]{:T(128)}) while((s32[]{:T(128)}, f32[256,256]{1,0:T(8,128)S(1)}, s32[2,2]{1,0:T(2,128)S(1)}, f32[2,128,128]{2,1,0:T(8,128)S(1)}, s32[]{:T(128)}) %tuple.30), condition=%wide.while_cond, body=%wide.while_body.sunk | while | flops 2 | bytes 131189 | solution.py:35
  110.2 0.6 fusion.35
  110.7 1.4 bitcast_dynamic-update-slice_fusion.2
  112.2 0.6 fusion.35
  112.7 1.4 bitcast_dynamic-update-slice_fusion.2
  114.1 19.7 %custom-call.19 = f32[2,128,128]{1,2,0:T(8,128)S(1)} custom-call(f32[2,128,128]{2,1,0:T(8,128)S(1)} %get-tuple-element.10), custom_call_target="InvertDiagBlocksLowerTriangular" | custom-call | tf_op jit(solution)/shard_map/jit(_cho_solve)/triangular_solve | solution.py:35
  133.8 0.3 fusion.9
  134.1 0.4 convolution_subtract_fusion.1
  134.5 0.3 fusion.16
  134.9 0.3 fusion.15
  135.1 0.3 convolution_subtract_fusion
  135.4 0.3 fusion.14
  135.7 0.8 copy.10
  136.6 0.0 copy-done
  136.6 0.0 copy-done.1
  136.6 1.0 multiply_reduce_fusion
  137.5 0.5 add_sqrt_fusion
  (12 shorter events, 0.2 us)
Async XLA Ops:
  7.2 129.4 %copy-start = (f32[3,256]{1,0:T(4,128)S(1)}, f32[3,256]{1,0:T(4,128)}, u32[]{:S(2)}) copy-start(f32[3,256]{1,0:T(4,128)} %param.6) | copy-start | bytes 9220
  7.2 129.4 %copy-start.1 = (f32[3]{0:T(128)S(1)}, f32[3]{0:T(128)}, u32[]{:S(2)}) copy-start(f32[3]{0:T(128)} %param.7) | copy-start | bytes 40
  7.2 56.6 %all-gather.3.cloned.1.call-start = ((), (), s32[]{:S(2)}) async-start(), calls=%async_computation | async-start | bytes 1179648 | tf_op jit(solution)/shard_map/all_gather | solution.py:25
Sparse Core Ops, SparseCore 0:
  20.8 42.9 all-gather.2
